TPU v7x, 32 devices: a whole 2x2x4 slice. The times are simulated.
32 devices in a mesh: groups: 2 (over y), tm: 4 (over z), rows: 4 (over x, core).
Axes of the slice: x: 2, y: 2, z: 4, core: 2. Of those that a mesh axis runs over, the one named last changes fastest.
Arguments:
- latents: bfloat16 [16, 16, 128, 256], P(('groups', 'tm'), 'rows'), parts along dimension 0, may hold values from -6 to 6
- weight_in: bfloat16 [3, 3, 256, 256], replicated, may hold values from -0.125 to 0.125
- weight_out: bfloat16 [3, 3, 256, 256], replicated, may hold values from -0.0234375 to 0.0234375
- decay_table: float32 [16], replicated, may hold values from 0.99 to 0.999
- decay_index: int32 [256], replicated, may hold values from 0 to 15
Outputs:
- updated: bfloat16 [16, 16, 128, 256], P(('groups', 'tm'), 'rows'), parts along dimension 0
There are 2 independent parts, one for each index of `groups`. A program takes and returns all parts, laid end to end along the dimension named above; an argument that names none is the same for every part. Nothing has to cross between parts.
All inputs are finite; a program needn't handle non-finite values.
Results may differ from a plain program's by a relative error of at most 0.0032.
Values may be sent and summed in bfloat16 or wider, within the bound.
A program may use at most 64 MiB of HBM per device.

v0:
```python
import jax
import jax.numpy as jnp
from jax import lax
from jax.sharding import PartitionSpec as P


def extended(block, sides, width):
    for axis, dim in sides:
        count = lax.axis_size(axis)
        forward = [(i, i + 1) for i in range(count - 1)]
        backward = [(target, source) for source, target in forward]
        low = lax.ppermute(
            lax.slice_in_dim(block, block.shape[dim] - width, None, axis=dim), axis, forward
        )
        high = lax.ppermute(lax.slice_in_dim(block, 0, width, axis=dim), axis, backward)
        block = jnp.concatenate([low, block, high], axis=dim)
    return block


def carried_in(value, axis, join, neutral):
    count, mine = (lax.axis_size(axis), lax.axis_index(axis))
    pieces = jax.tree.map(lambda part: lax.all_gather(part, axis), value)
    so_far = jax.tree.map(
        lambda part, zero: jnp.full_like(part, 0) + jnp.asarray(zero, part.dtype), value, neutral
    )

    def hop(position, so_far):
        longer = join(so_far, jax.tree.map(lambda part: part[position], pieces))
        return jax.tree.map(lambda new, old: jnp.where(position < mine, new, old), longer, so_far)

    return lax.fori_loop(0, count - 1, hop, so_far)


def convolve(padded, weight, count):
    frames = padded.shape[0]
    width = padded.shape[2]
    depth = weight.shape[2]
    widened = jnp.pad(padded, ((0, 0), (0, 0), (1, 1), (0, 0)))
    total = jnp.zeros((frames * count * width, weight.shape[3]), jnp.float32)
    for tap_row in range(3):
        for tap_col in range(3):
            window = widened[:, tap_row : tap_row + count, tap_col : tap_col + width, :].reshape(
                -1, depth
            )
            total = total + jnp.dot(
                window, weight[tap_row, tap_col], preferred_element_type=jnp.float32
            )
    return total.reshape(frames, count, width, weight.shape[3])


def combine(earlier, later):
    return (earlier[0] * later[0], later[0] * earlier[1] + later[1])


def local_states(driven, decays):
    running = jnp.zeros(driven.shape[1:], jnp.float32)
    gathered = []
    for moment in range(driven.shape[0]):
        running = decays * running + driven[moment]
        gathered.append(running)
    return (jnp.stack(gathered), running)


def finish(partial_value, carried_state, decays):
    frames = partial_value.shape[0]
    growth = decays[None, :] ** jnp.arange(1, frames + 1, dtype=jnp.float32)[:, None]
    return partial_value + growth[:, None, None, :] * carried_state[None]


def local(latents, weight_in, weight_out, decay_table, decay_index):
    frames, strip, width, channels = latents.shape
    levels = decay_table.shape[0]
    onehot = decay_index[:, None] == jnp.arange(levels, dtype=jnp.int32)[None, :]
    decays = jnp.sum(jnp.where(onehot, decay_table[None, :], 0.0), axis=1)
    powers = decays ** float(frames)
    padded = extended(latents, (("rows", 1),), 1)
    driven = convolve(padded, weight_in, strip)
    partial_value, last_state = local_states(driven, decays)
    identity = (jnp.ones_like(decays), jnp.zeros(last_state.shape, jnp.float32))
    _, carried = carried_in((powers, last_state), "tm", combine, identity)
    rounded = finish(partial_value, carried, decays).astype(jnp.bfloat16)
    padded_states = extended(rounded, (("rows", 1),), 1)
    mixed = convolve(padded_states, weight_out, strip)
    return (latents.astype(jnp.float32) + jax.nn.gelu(mixed)).astype(jnp.bfloat16)


def solution(mesh):
    in_specs = (P(("groups", "tm"), "rows", None, None), P(), P(), P(), P())
    out_specs = P(("groups", "tm"), "rows", None, None)
    return jax.shard_map(local, mesh=mesh, in_specs=in_specs, out_specs=out_specs, check_vma=False)
```

profile of v0, /device:TPU:1, one launch (start us, length us, event | category | flops | bytes accessed | tf_op | source)
XLA Modules:
  0.0 98.0 jit_solution(2424338155233784217)
XLA Ops:
  6.5 1.0 %fusion.63 = (bf16[2,1,128,256]{3,2,1,0:T(8,128)(2,1)S(1)}, bf16[2,1,128,256]{3,2,1,0:T(8,128)(2,1)S(1)}) fusion(bf16[2,4,128,256]{3,2,1,0:T(8,128)(2,1)} %param.7), kind=kLoop, calls=%fused_computation.97 | loop fusion | bytes 524288 | tf_op jit(solution)/shard_map/slice | solution.py:13
  7.5 4.5 %collective-permute-start = (bf16[2,1,128,256]{3,2,1,0:T(8,128)(2,1)S(1)}, bf16[2,1,128,256]{3,2,1,0:T(8,128)(2,1)S(1)}, u32[]{:S(2)}, u32[]{:S(2)}) collective-permute-start(bf16[2,1,128,256]{3,2,1,0:T(8,128)(2,1)S(1)} %get-tuple-element.150), channel_id=1, source_target_pairs={{0,1},{1,2},{2,3},{4,5},{5,6},{6,7},{8,9},{9,10},{10,11},{12,13},{... | collective-permute-start | bytes 393224 | tf_op jit(solution)/shard_map/ppermute | solution.py:12
  12.0 1.9 %collective-permute-start.1 = (bf16[2,1,128,256]{3,2,1,0:T(8,128)(2,1)S(1)}, bf16[2,1,128,256]{3,2,1,0:T(8,128)(2,1)S(1)}, u32[]{:S(2)}, u32[]{:S(2)}) collective-permute-start(bf16[2,1,128,256]{3,2,1,0:T(8,128)(2,1)S(1)} %get-tuple-element.151), channel_id=1, source_target_pairs={{1,0},{2,1},{3,2},{5,4},{6,5},{7,6},{9,8},{10,9},{11,10},{13,12},{... | collective-permute-start | bytes 393224 | tf_op jit(solution)/shard_map/ppermute | solution.py:15
  14.0 0.8 select_reduce_fusion
  14.8 3.6 %collective-permute-done.1 = bf16[2,1,128,256]{3,2,1,0:T(8,128)(2,1)S(1)} collective-permute-done((bf16[2,1,128,256]{3,2,1,0:T(8,128)(2,1)S(1)}, bf16[2,1,128,256]{3,2,1,0:T(8,128)(2,1)S(1)}, u32[]{:S(2)}, u32[]{:S(2)}) %collective-permute-start.1) | collective-permute-done | bytes 131104 | tf_op jit(solution)/shard_map/ppermute | solution.py:15
  18.3 1.3 %fusion.18 = bf16[2,6,130,256]{3,2,1,0:T(8,128)(2,1)S(1)} fusion(bf16[2,1,128,256]{3,2,1,0:T(8,128)(2,1)S(1)} %collective-permute-done.1, bf16[2,4,128,256]{3,2,1,0:T(8,128)(2,1)} %param.7, bf16[2,1,128,256]{3,2,1,0:T(8,128)(2,1)S(1)} %collective-permute-done), kind=kLoop, calls=%fused_computation.40 | loop fusion | flops 4792320 | bytes 1585152 | tf_op jit(solution)/shard_map/concatenate | solution.py:16
  19.6 0.4 fusion.61
  20.0 0.8 copy-done.2
  20.9 0.3 fusion.39
  21.2 0.3 fusion.30
  21.5 0.7 copy-done
  22.9 0.3 convolution_add_fusion.11
  23.2 0.3 convolution_add_fusion.10
  23.5 0.3 convolution_add_fusion.9
  23.8 0.3 convolution_add_fusion.8
  24.5 0.9 multiply_add_fusion
  25.4 9.2 %all-gather.1 = f32[4,1,256]{2,1,0:T(1,128)S(1)} all-gather(f32[1,1,256]{2,1,0:T(1,128)S(1)} %bitcast.129), channel_id=2, replica_groups=mesh['groups'=2,'tm'=4,'rows'=4] {'tm'}, dimensions={0}, use_global_device_ids=true | all-gather | bytes 5120 | tf_op jit(solution)/shard_map/all_gather | solution.py:22
  34.7 36.2 %all-gather.4.cloned.1.call-done = f32[4,4,128,256]{3,2,1,0:T(8,128)} async-done(((f32[1,4,128,256]{3,2,1,0:T(8,128)}), f32[4,4,128,256]{3,2,1,0:T(8,128)}) %all-gather.4.cloned.1.call-update) | async-done | bytes 2097168 | tf_op jit(solution)/shard_map/all_gather | solution.py:22
  70.8 4.6 %while.14 = (s32[]{:T(128)}, f32[4,128,256]{2,1,0:T(8,128)S(1)}, s32[]{:T(128)}, f32[4,256]{1,0:T(4,128)S(1)}, f32[4,4,128,256]{3,2,1,0:T(8,128)}, /*index=5*/s32[]{:T(128)}, s32[]{:T(128)}) while((s32[]{:T(128)}, f32[4,128,256]{2,1,0:T(8,128)S(1)}, s32[]{:T(128)}, f32[4,256]{1,0:T(4,128)S(1)}, f32[4,4,128,256]{3,2,1,0:T(8,128)}, ...), condition=%wide.region_2.3_spmd.clone, body=%wide.region_1.2_spmd.clone.sunk | while | flops 524292 | bytes 1576041 | solution.py:31
  70.9 1.5 %fusion.83 = f32[4,128,256]{2,1,0:T(8,128)S(1)} fusion(f32[4,4,128,256]{3,2,1,0:T(8,128)} %get-tuple-element.203, s32[]{:T(128)} %get-tuple-element.192, f32[4,128,256]{2,1,0:T(8,128)S(1)} %get-tuple-element.193, f32[256]{0:T(256)S(1)} %bitcast.127, pred[]{:T(512)S(6)} %compare.55, pred[]{:T(512)S(6)} %lt.22), kind=kLoop, calls=%fused_computation.1.clone.1 | loop fusion | flops 524288 | bytes 1573894 | tf_op jit(solution)/shard_map/while/body/eval_jaxpr/jit(_where)/select_n | solution.py:29
  72.4 1.5 %fusion.83 = f32[4,128,256]{2,1,0:T(8,128)S(1)} fusion(f32[4,4,128,256]{3,2,1,0:T(8,128)} %get-tuple-element.203, s32[]{:T(128)} %get-tuple-element.192, f32[4,128,256]{2,1,0:T(8,128)S(1)} %get-tuple-element.193, f32[256]{0:T(256)S(1)} %bitcast.127, pred[]{:T(512)S(6)} %compare.55, pred[]{:T(512)S(6)} %lt.22), kind=kLoop, calls=%fused_computation.1.clone.1 | loop fusion | flops 524288 | bytes 1573894 | tf_op jit(solution)/shard_map/while/body/eval_jaxpr/jit(_where)/select_n | solution.py:29
  73.9 1.5 %fusion.83 = f32[4,128,256]{2,1,0:T(8,128)S(1)} fusion(f32[4,4,128,256]{3,2,1,0:T(8,128)} %get-tuple-element.203, s32[]{:T(128)} %get-tuple-element.192, f32[4,128,256]{2,1,0:T(8,128)S(1)} %get-tuple-element.193, f32[256]{0:T(256)S(1)} %bitcast.127, pred[]{:T(512)S(6)} %compare.55, pred[]{:T(512)S(6)} %lt.22), kind=kLoop, calls=%fused_computation.1.clone.1 | loop fusion | flops 524288 | bytes 1573894 | tf_op jit(solution)/shard_map/while/body/eval_jaxpr/jit(_where)/select_n | solution.py:29
  75.6 3.8 %collective-permute-start.2 = (bf16[2,1,128,256]{3,2,1,0:T(8,128)(2,1)S(1)}, bf16[2,1,128,256]{3,2,1,0:T(8,128)(2,1)S(1)}, u32[]{:S(2)}, u32[]{:S(2)}) collective-permute-start(bf16[2,1,128,256]{3,2,1,0:T(8,128)(2,1)S(1)} %get-tuple-element.146), channel_id=1, source_target_pairs={{0,1},{1,2},{2,3},{4,5},{5,6},{6,7},{8,9},{9,10},{10,11},{12,13},{... | collective-permute-start | bytes 393224 | tf_op jit(solution)/shard_map/ppermute | solution.py:12
  79.4 1.9 %collective-permute-start.3 = (bf16[2,1,128,256]{3,2,1,0:T(8,128)(2,1)S(1)}, bf16[2,1,128,256]{3,2,1,0:T(8,128)(2,1)S(1)}, u32[]{:S(2)}, u32[]{:S(2)}) collective-permute-start(bf16[2,1,128,256]{3,2,1,0:T(8,128)(2,1)S(1)} %get-tuple-element.147), channel_id=1, source_target_pairs={{1,0},{2,1},{3,2},{5,4},{6,5},{7,6},{9,8},{10,9},{11,10},{13,12},{... | collective-permute-start | bytes 393224 | tf_op jit(solution)/shard_map/ppermute | solution.py:15
  81.4 4.3 %collective-permute-done.3 = bf16[2,1,128,256]{3,2,1,0:T(8,128)(2,1)S(1)} collective-permute-done((bf16[2,1,128,256]{3,2,1,0:T(8,128)(2,1)S(1)}, bf16[2,1,128,256]{3,2,1,0:T(8,128)(2,1)S(1)}, u32[]{:S(2)}, u32[]{:S(2)}) %collective-permute-start.3) | collective-permute-done | bytes 131104 | tf_op jit(solution)/shard_map/ppermute | solution.py:15
  86.0 0.4 fusion.60
  86.4 0.8 copy-done.3
  87.5 0.3 fusion.19
  87.9 0.3 convolution_add_fusion.6
  88.8 0.3 convolution_add_fusion.3
  89.7 0.3 fusion.2
  90.0 1.2 %fusion.12 = bf16[2,4,128,256]{3,2,1,0:T(8,128)(2,1)} fusion(f32[2,4,128,256]{3,2,1,0:T(8,128)S(1)} %bitcast.108, bf16[2,4,128,256]{3,2,1,0:T(8,128)(2,1)S(1)} %copy-done), kind=kLoop, calls=%fused_computation.31 | loop fusion | flops 2883584 | bytes 2097152 | tf_op jit(solution)/shard_map/convert_element_type | solution.py:84
  (31 shorter events, 3.1 us)
Async XLA Ops:
  6.5 64.3 %all-gather.4.cloned.1.call-start = ((), (), s32[]{:S(2)}) async-start(), calls=%async_computation | async-start | bytes 2621440 | tf_op jit(solution)/shard_map/all_gather | solution.py:22
  7.5 7.2 %collective-permute-start = (bf16[2,1,128,256]{3,2,1,0:T(8,128)(2,1)S(1)}, bf16[2,1,128,256]{3,2,1,0:T(8,128)(2,1)S(1)}, u32[]{:S(2)}, u32[]{:S(2)}) collective-permute-start(bf16[2,1,128,256]{3,2,1,0:T(8,128)(2,1)S(1)} %get-tuple-element.150), channel_id=1, source_target_pairs={{0,1},{1,2},{2,3},{4,5},{5,6},{6,7},{8,9},{9,10},{10,11},{12,13},{... | collective-permute-start | bytes 393224 | tf_op jit(solution)/shard_map/ppermute | solution.py:12
  12.0 6.3 %collective-permute-start.1 = (bf16[2,1,128,256]{3,2,1,0:T(8,128)(2,1)S(1)}, bf16[2,1,128,256]{3,2,1,0:T(8,128)(2,1)S(1)}, u32[]{:S(2)}, u32[]{:S(2)}) collective-permute-start(bf16[2,1,128,256]{3,2,1,0:T(8,128)(2,1)S(1)} %get-tuple-element.151), channel_id=1, source_target_pairs={{1,0},{2,1},{3,2},{5,4},{6,5},{7,6},{9,8},{10,9},{11,10},{13,12},{... | collective-permute-start | bytes 393224 | tf_op jit(solution)/shard_map/ppermute | solution.py:15
  19.6 1.3 %copy-start.2 = (bf16[3,3,256,256]{3,2,1,0:T(8,128)(2,1)S(1)}, bf16[3,3,256,256]{3,2,1,0:T(8,128)(2,1)}, u32[]{:S(2)}) copy-start(bf16[3,3,256,256]{3,2,1,0:T(8,128)(2,1)} %param.8) | copy-start | bytes 3538948
  21.2 1.0 %copy-start = (bf16[2,4,128,256]{3,2,1,0:T(8,128)(2,1)S(1)}, bf16[2,4,128,256]{3,2,1,0:T(8,128)(2,1)}, u32[]{:S(2)}) copy-start(bf16[2,4,128,256]{3,2,1,0:T(8,128)(2,1)} %param.7) | copy-start | bytes 1572868
  70.8 4.6 %copy-start.1 = (f32[1,4,128,256]{3,2,1,0:T(8,128)S(1)}, f32[1,4,128,256]{3,2,1,0:T(8,128)}, u32[]{:S(2)}) copy-start(f32[1,4,128,256]{3,2,1,0:T(8,128)} %get-tuple-element.128) | copy-start | bytes 1572868
  75.6 5.8 %collective-permute-start.2 = (bf16[2,1,128,256]{3,2,1,0:T(8,128)(2,1)S(1)}, bf16[2,1,128,256]{3,2,1,0:T(8,128)(2,1)S(1)}, u32[]{:S(2)}, u32[]{:S(2)}) collective-permute-start(bf16[2,1,128,256]{3,2,1,0:T(8,128)(2,1)S(1)} %get-tuple-element.146), channel_id=1, source_target_pairs={{0,1},{1,2},{2,3},{4,5},{5,6},{6,7},{8,9},{9,10},{10,11},{12,13},{... | collective-permute-start | bytes 393224 | tf_op jit(solution)/shard_map/ppermute | solution.py:12
  79.4 6.3 %collective-permute-start.3 = (bf16[2,1,128,256]{3,2,1,0:T(8,128)(2,1)S(1)}, bf16[2,1,128,256]{3,2,1,0:T(8,128)(2,1)S(1)}, u32[]{:S(2)}, u32[]{:S(2)}) collective-permute-start(bf16[2,1,128,256]{3,2,1,0:T(8,128)(2,1)S(1)} %get-tuple-element.147), channel_id=1, source_target_pairs={{1,0},{2,1},{3,2},{5,4},{6,5},{7,6},{9,8},{10,9},{11,10},{13,12},{... | collective-permute-start | bytes 393224 | tf_op jit(solution)/shard_map/ppermute | solution.py:15
  85.9 1.3 %copy-start.3 = (bf16[3,3,256,256]{3,2,1,0:T(8,128)(2,1)S(1)}, bf16[3,3,256,256]{3,2,1,0:T(8,128)(2,1)}, u32[]{:S(2)}) copy-start(bf16[3,3,256,256]{3,2,1,0:T(8,128)(2,1)} %param.9) | copy-start | bytes 3538948
Sparse Core Ops, SparseCore 0:
  25.5 45.2 all-gather.3
where the time goes:
time: 98.5 us; the launch traced here: 98 us
  waiting for transfers between devices  44.1 us (45%)
  between operations  13.7 us (14%)
  starting transfers between devices  12.2 us (12%)
  other arithmetic  9.16 us (9%)
  blocking collectives  9.16 us (9%)
  matrix products  5.29 us (5%)
  local copies, waits for them, and re-layouts  4.44 us (5%)
    all_gather x1, waiting for transfers between devices, carried_in(): pieces = jax.tree.map(lambda part: lax.all_gather(part, axis), value)  36.2 us
    all_gather x1, blocking collectives, carried_in(): pieces = jax.tree.map(lambda part: lax.all_gather(part, axis), value)  9.16 us
    ppermute x2, starting transfers between devices, extended(): lax.ppermute(lax.slice_in_dim(block, block.shape[dim] - width, None, axis...  8.32 us
    ppermute x2, waiting for transfers between devices, extended(): lax.ppermute(lax.slice_in_dim(block, 0, width, axis=dim), axis, backward)  7.91 us
    dot_general x18, matrix products, convolve(): jnp.dot(window, weight[tap_row, tap_col], preferred_element_type=jnp.floa...  5.29 us
    select_n x3, other arithmetic, hop(): jnp.where(position < mine, new, old)  4.49 us
    ppermute x2, starting transfers between devices, extended(): lax.ppermute(lax.slice_in_dim(block, 0, width, axis=dim), axis, backward)  3.84 us
    unnamed x9, local copies, waits for them, and re-layouts  2.4 us
  transfers between devices with their start and end apart: 5, of which 3 were waited for; matrix products, arithmetic and copies ran while one was open for 1% of the time, Pallas kernels for 0%

commit v1 on v0

v1 whole, which is shorter than its diff:
```python
import functools

import jax
import jax.numpy as jnp
from jax import lax
from jax.experimental import pallas as pl
from jax.experimental.pallas import tpu as pltpu
from jax.sharding import PartitionSpec as P

MESH = pl.DeviceIdType.MESH
PIECES = 2


def kernel(
    positions,
    strips,
    lat_hbm,
    win_hbm,
    wout_hbm,
    table_ref,
    index_ref,
    out_hbm,
    lat,
    win,
    wout,
    halo,
    wide,
    partial,
    carry,
    passed,
    rounded,
    state_halo,
    wide_states,
    result,
    load_sem,
    store_sem,
    halo_send,
    halo_recv,
    state_send,
    state_recv,
    carry_send,
    carry_recv,
):
    frames, strip, width, channels = lat.shape
    row = lax.axis_index("rows")
    moment = lax.axis_index("tm")
    has_up, has_down = row > 0, row < strips - 1
    has_before, has_after = moment > 0, moment < positions - 1
    span = width // PIECES

    load_lat = pltpu.make_async_copy(lat_hbm, lat, load_sem.at[0])
    load_win = pltpu.make_async_copy(win_hbm, win, load_sem.at[1])
    load_wout = pltpu.make_async_copy(wout_hbm, wout, load_sem.at[2])
    load_lat.start()
    load_win.start()
    load_wout.start()

    barrier = pltpu.get_barrier_semaphore()
    near = (
        (has_up, {"rows": row - 1}),
        (has_down, {"rows": row + 1}),
        (has_before, {"tm": moment - 1}),
        (has_after, {"tm": moment + 1}),
    )
    total = 0
    for exists, where in near:
        total = total + exists.astype(jnp.int32)

        @pl.when(exists)
        def _():
            pl.semaphore_signal(barrier, inc=1, device_id=where, device_id_type=MESH)

    pl.semaphore_wait(barrier, total)

    def halo_copy(side):
        source = lat_hbm.at[:, strip - 1] if side == 0 else lat_hbm.at[:, 0]
        target = row + 1 if side == 0 else row - 1
        return pltpu.make_async_remote_copy(
            src_ref=source,
            dst_ref=halo.at[side],
            send_sem=halo_send.at[side],
            recv_sem=halo_recv.at[side],
            device_id={"rows": target},
            device_id_type=MESH,
        )

    def state_copy(side):
        source = rounded.at[strip - 1] if side == 0 else rounded.at[0]
        target = row + 1 if side == 0 else row - 1
        return pltpu.make_async_remote_copy(
            src_ref=source,
            dst_ref=state_halo.at[side],
            send_sem=state_send.at[side],
            recv_sem=state_recv.at[side],
            device_id={"rows": target},
            device_id_type=MESH,
        )

    def carry_copy(i, piece):
        part = pl.ds(piece * span, span)
        return pltpu.make_async_remote_copy(
            src_ref=passed.at[i, part],
            dst_ref=carry.at[i, part],
            send_sem=carry_send.at[i, piece],
            recv_sem=carry_recv.at[i, piece],
            device_id={"tm": moment + 1},
            device_id_type=MESH,
        )

    @pl.when(has_down)
    def _():
        halo_copy(0).start()

    @pl.when(has_up)
    def _():
        halo_copy(1).start()

    chosen = index_ref[...]
    decays = jnp.zeros(chosen.shape, jnp.float32)
    for level in range(table_ref.shape[0]):
        decays = jnp.where(chosen == level, table_ref[level], decays)
    growth = [decays]
    for _ in range(frames - 1):
        growth.append(growth[-1] * decays)

    column = lax.broadcasted_iota(jnp.int32, (width, channels), 0)

    def spread(target, place, frame, value):
        full = value.astype(jnp.float32)
        before = jnp.where(column == 0, 0.0, pltpu.roll(full, 1, 0))
        after = jnp.where(column == width - 1, 0.0, pltpu.roll(full, width - 1, 0))
        target[place, frame, :, 0:channels] = before.astype(jnp.bfloat16)
        target[place, frame, :, channels : 2 * channels] = value
        target[place, frame, :, 2 * channels : 3 * channels] = after.astype(jnp.bfloat16)

    def border(target, place, buffer, side, exists, arrival):
        @pl.when(exists)
        def _():
            arrival.wait_recv()
            for frame in range(frames):
                spread(target, place, frame, buffer[side, frame])

        @pl.when(jnp.logical_not(exists))
        def _():
            target[place] = jnp.zeros(target.shape[1:], target.dtype)

    def convolve(source, weight, i):
        window = jnp.concatenate([source[i], source[i + 1], source[i + 2]], axis=-1)
        flat = window.reshape(frames * width, 9 * channels)
        return jnp.dot(flat, weight[...], preferred_element_type=jnp.float32).reshape(
            frames, width, channels
        )

    def drive(i):
        driven = convolve(wide, win, i)
        running = driven[0]
        partial[i, 0] = running
        for frame in range(1, frames):
            running = decays * running + driven[frame]
            partial[i, frame] = running

    def publish(i):
        for side, edge in ((0, strip - 1), (1, 0)):
            if i == edge:

                @pl.when(has_down if side == 0 else has_up)
                def _():
                    state_copy(side).start()

        for frame in range(frames):
            spread(wide_states, i + 1, frame, rounded[i, frame])

    def first(i):
        @pl.when(jnp.logical_not(has_before))
        def _():
            passed[i] = partial[i, frames - 1].astype(passed.dtype)

            @pl.when(has_after)
            def _():
                for piece in range(PIECES):
                    carry_copy(i, piece).start()

            for frame in range(frames):
                rounded[i, frame] = partial[i, frame].astype(jnp.bfloat16)
            publish(i)

    def later(i):
        @pl.when(has_before)
        def _():
            for piece in range(PIECES):
                part = pl.ds(piece * span, span)
                carry_copy(i, piece).wait_recv()
                arrived = carry[i, part].astype(jnp.float32)
                last = partial[i, frames - 1, part] + growth[frames - 1] * arrived
                passed[i, part] = last.astype(passed.dtype)

                @pl.when(has_after)
                def _():
                    carry_copy(i, piece).start()

                rounded[i, frames - 1, part] = last.astype(jnp.bfloat16)
                for frame in range(frames - 1):
                    state = partial[i, frame, part] + growth[frame] * arrived
                    rounded[i, frame, part] = state.astype(jnp.bfloat16)
            publish(i)

    def emit(i):
        mixed = convolve(wide_states, wout, i)
        for frame in range(frames):
            updated = lat[frame, i].astype(jnp.float32) + jax.nn.gelu(mixed[frame])
            result[frame, i] = updated.astype(jnp.bfloat16)
        pltpu.make_async_copy(result.at[:, i], out_hbm.at[:, i], store_sem.at[i]).start()

    middle = list(range(1, strip - 1))
    edges = [0, strip - 1]

    load_lat.wait()
    for i in range(strip):
        for frame in range(frames):
            spread(wide, i + 1, frame, lat[frame, i])
    load_win.wait()
    for i in middle:
        drive(i)
        first(i)
    border(wide, 0, halo, 0, has_up, halo_copy(0))
    drive(0)
    first(0)
    border(wide, strip + 1, halo, 1, has_down, halo_copy(1))
    drive(strip - 1)
    first(strip - 1)
    load_wout.wait()
    for i in middle + edges:
        later(i)
    for i in middle:
        emit(i)
    border(wide_states, 0, state_halo, 0, has_up, state_copy(0))
    emit(0)
    border(wide_states, strip + 1, state_halo, 1, has_down, state_copy(1))
    emit(strip - 1)

    @pl.when(has_down)
    def _():
        halo_copy(0).wait_send()
        state_copy(0).wait_send()

    @pl.when(has_up)
    def _():
        halo_copy(1).wait_send()
        state_copy(1).wait_send()

    @pl.when(has_after)
    def _():
        for i in range(strip):
            for piece in range(PIECES):
                carry_copy(i, piece).wait_send()

    for i in range(strip):
        pltpu.make_async_copy(result.at[:, i], out_hbm.at[:, i], store_sem.at[i]).wait()


def local(positions, strips, latents, weight_in, weight_out, decay_table, decay_index):
    frames, strip, width, channels = latents.shape
    link = jnp.bfloat16 if positions <= 8 else jnp.float32
    half = jnp.bfloat16
    dma = pltpu.SemaphoreType.DMA
    anywhere = pl.BlockSpec(memory_space=pl.ANY)
    return pl.pallas_call(
        functools.partial(kernel, positions, strips),
        out_shape=jax.ShapeDtypeStruct(latents.shape, latents.dtype),
        in_specs=[
            anywhere,
            anywhere,
            anywhere,
            pl.BlockSpec(memory_space=pltpu.SMEM),
            pl.BlockSpec(memory_space=pltpu.VMEM),
        ],
        out_specs=anywhere,
        scratch_shapes=[
            pltpu.VMEM((frames, strip, width, channels), half),
            pltpu.VMEM((9 * channels, channels), half),
            pltpu.VMEM((9 * channels, channels), half),
            pltpu.VMEM((2, frames, width, channels), half),
            pltpu.VMEM((strip + 2, frames, width, 3 * channels), half),
            pltpu.VMEM((strip, frames, width, channels), jnp.float32),
            pltpu.VMEM((strip, width, channels), link),
            pltpu.VMEM((strip, width, channels), link),
            pltpu.VMEM((strip, frames, width, channels), half),
            pltpu.VMEM((2, frames, width, channels), half),
            pltpu.VMEM((strip + 2, frames, width, 3 * channels), half),
            pltpu.VMEM((frames, strip, width, channels), half),
            dma((3,)),
            dma((strip,)),
            dma((2,)),
            dma((2,)),
            dma((2,)),
            dma((2,)),
            dma((strip, PIECES)),
            dma((strip, PIECES)),
        ],
        compiler_params=pltpu.CompilerParams(collective_id=0, has_side_effects=True),
    )(
        latents,
        weight_in.reshape(9 * channels, channels),
        weight_out.reshape(9 * channels, channels),
        decay_table,
        decay_index.reshape(1, channels),
    )


def solution(mesh):
    in_specs = (P(("groups", "tm"), "rows", None, None), P(), P(), P(), P())
    out_specs = P(("groups", "tm"), "rows", None, None)
    body = functools.partial(local, mesh.shape["tm"], mesh.shape["rows"])
    return jax.shard_map(body, mesh=mesh, in_specs=in_specs, out_specs=out_specs, check_vma=False)
```

time: 98.5 us -> 23.8 us (0.24)
  the two profiles are of different devices: /device:TPU:1 before, /device:TPU:26 now
where the time goes in v1:
time: 23.8 us; the launch traced here: 23.6 us
  Pallas kernels  21.7 us (91%)
  local copies, waits for them, and re-layouts  1.87 us (8%)
    pallas_call x1, Pallas kernels, local(): pl.pallas_call(functools.partial(kernel, positions, strips), out_shape=ja...  21.7 us
    unnamed x1, local copies, waits for them, and re-layouts  1.87 us

profile of v1, /device:TPU:26, one launch (start us, length us, event | category | flops | bytes accessed | tf_op | source)
XLA Modules:
  0.0 23.6 jit_solution(16911102045564329054)
XLA Ops:
  0.0 21.7 %shard_map.55 = bf16[2,4,128,256]{3,2,1,0:T(8,128)(2,1)} custom-call(bf16[2,4,128,256]{3,2,1,0:T(8,128)(2,1)} %lat_hbm.1, bf16[2304,256]{1,0:T(8,128)(2,1)} %bitcast.3, bf16[2304,256]{1,0:T(8,128)(2,1)} %bitcast.4, f32[16]{0:T(128)} %table_ref.1, s32[1,256]{1,0:T(1,128)} %bitcast.5), custom_call_target="tpu_custom_call" | custom-call | tf_op jit(solution)/shard_map/pallas_call | solution.py:267
  21.7 1.9 %copy.7 = bf16[2,4,128,256]{3,2,1,0:T(8,128)(2,1)} copy(bf16[2,4,128,256]{3,2,1,0:T(8,128)(2,1)} %shard_map.55) | data formatting | bytes 1048576

commit v2 on v1

--- a/solution.py
+++ b/solution.py
@@ -268,9 +268,9 @@
         functools.partial(kernel, positions, strips),
         out_shape=jax.ShapeDtypeStruct(latents.shape, latents.dtype),
         in_specs=[
-            anywhere,
-            anywhere,
-            anywhere,
+            pl.BlockSpec(memory_space=pltpu.HBM),
+            pl.BlockSpec(memory_space=pltpu.HBM),
+            pl.BlockSpec(memory_space=pltpu.HBM),
             pl.BlockSpec(memory_space=pltpu.SMEM),
             pl.BlockSpec(memory_space=pltpu.VMEM),
         ],
@@ -297,7 +297,7 @@
             dma((strip, PIECES)),
             dma((strip, PIECES)),
         ],
-        compiler_params=pltpu.CompilerParams(collective_id=0, has_side_effects=True),
+        compiler_params=pltpu.CompilerParams(collective_id=0, has_side_effects=True, vmem_limit_bytes=32 * 1024 * 1024),
     )(
         latents,
         weight_in.reshape(9 * channels, channels),

time: 23.8 us -> 27.6 us (1.16)
  local copies, waits for them, and re-layouts: 1.87 us -> 5.71 us
    unnamed x1 -> x11, local copies, waits for them, and re-layouts: 1.87 us -> 5.71 us
where the time goes in v2:
time: 27.6 us; the launch traced here: 27.4 us
  Pallas kernels  21.6 us (78%)
  local copies, waits for them, and re-layouts  5.71 us (21%)
    pallas_call x1, Pallas kernels, local(): pl.pallas_call(functools.partial(kernel, positions, strips), out_shape=ja...  21.6 us
    unnamed x11, local copies, waits for them, and re-layouts  5.71 us

profile of v2, /device:TPU:26, one launch (start us, length us, event | category | flops | bytes accessed | tf_op | source)
XLA Modules:
  0.0 27.4 jit_solution(6084558740548963075)
XLA Ops:
  0.0 0.0 copy-start
  0.0 1.3 %copy-done = bf16[3,3,256,256]{3,2,1,0:T(8,128)(2,1)S(1)} copy-done((bf16[3,3,256,256]{3,2,1,0:T(8,128)(2,1)S(1)}, bf16[3,3,256,256]{3,2,1,0:T(8,128)(2,1)}, u32[]{:S(2)}) %copy-start) | copy-done | bytes 1179672
  1.3 0.0 copy-start.1
  1.3 1.3 %copy-done.1 = bf16[3,3,256,256]{3,2,1,0:T(8,128)(2,1)S(1)} copy-done((bf16[3,3,256,256]{3,2,1,0:T(8,128)(2,1)S(1)}, bf16[3,3,256,256]{3,2,1,0:T(8,128)(2,1)}, u32[]{:S(2)}) %copy-start.1) | copy-done | bytes 1179672
  2.5 0.0 copy-start.2
  2.5 1.0 %copy-done.2 = bf16[2,4,128,256]{3,2,1,0:T(8,128)(2,1)S(1)} copy-done((bf16[2,4,128,256]{3,2,1,0:T(8,128)(2,1)S(1)}, bf16[2,4,128,256]{3,2,1,0:T(8,128)(2,1)}, u32[]{:S(2)}) %copy-start.2) | copy-done | bytes 524312
  3.6 0.0 copy-start.3
  3.6 0.7 %copy-done.3 = s32[256]{0:T(256)S(1)} copy-done((s32[256]{0:T(256)S(1)}, s32[256]{0:T(256)}, u32[]{:S(2)}) %copy-start.3) | copy-done | bytes 1048
  4.3 0.0 copy-start.4
  4.3 0.7 %copy-done.4 = f32[16]{0:T(128)S(1)} copy-done((f32[16]{0:T(128)S(1)}, f32[16]{0:T(128)}, u32[]{:S(2)}) %copy-start.4) | copy-done | bytes 88
  4.9 21.6 %shard_map.55 = bf16[2,4,128,256]{3,2,1,0:T(8,128)(2,1)S(1)} custom-call(bf16[2,4,128,256]{3,2,1,0:T(8,128)(2,1)S(1)} %copy-done.2, bf16[2304,256]{1,0:T(8,128)(2,1)S(1)} %bitcast.3, bf16[2304,256]{1,0:T(8,128)(2,1)S(1)} %bitcast.4, f32[16]{0:T(128)S(1)} %copy-done.4, s32[1,256]{1,0:T(1,128)S(1)} %bitcast.5), custom_call_target="tpu_custom_call" | custom-call | tf_op jit(solution)/shard_map/pallas_call | solution.py:267
  26.6 0.8 %copy.7 = bf16[2,4,128,256]{3,2,1,0:T(8,128)(2,1)} copy(bf16[2,4,128,256]{3,2,1,0:T(8,128)(2,1)S(1)} %shard_map.55) | data formatting | bytes 1048576
Async XLA Ops:
  0.0 1.3 %copy-start = (bf16[3,3,256,256]{3,2,1,0:T(8,128)(2,1)S(1)}, bf16[3,3,256,256]{3,2,1,0:T(8,128)(2,1)}, u32[]{:S(2)}) copy-start(bf16[3,3,256,256]{3,2,1,0:T(8,128)(2,1)} %param.6) | copy-start | bytes 3538948
  1.3 1.3 %copy-start.1 = (bf16[3,3,256,256]{3,2,1,0:T(8,128)(2,1)S(1)}, bf16[3,3,256,256]{3,2,1,0:T(8,128)(2,1)}, u32[]{:S(2)}) copy-start(bf16[3,3,256,256]{3,2,1,0:T(8,128)(2,1)} %param.7) | copy-start | bytes 3538948
  2.5 1.0 %copy-start.2 = (bf16[2,4,128,256]{3,2,1,0:T(8,128)(2,1)S(1)}, bf16[2,4,128,256]{3,2,1,0:T(8,128)(2,1)}, u32[]{:S(2)}) copy-start(bf16[2,4,128,256]{3,2,1,0:T(8,128)(2,1)} %lat_hbm.1) | copy-start | bytes 1572868
  3.6 0.7 %copy-start.3 = (s32[256]{0:T(256)S(1)}, s32[256]{0:T(256)}, u32[]{:S(2)}) copy-start(s32[256]{0:T(256)} %param.9) | copy-start | bytes 3076
  4.3 0.7 %copy-start.4 = (f32[16]{0:T(128)S(1)}, f32[16]{0:T(128)}, u32[]{:S(2)}) copy-start(f32[16]{0:T(128)} %table_ref.1) | copy-start | bytes 196

commit v3 on v1

--- a/solution.py
+++ b/solution.py
@@ -30,6 +30,8 @@
     passed,
     rounded,
     state_halo,
+    relayed,
+    mixed,
     wide_states,
     result,
     load_sem,
@@ -40,6 +42,8 @@
     state_recv,
     carry_send,
     carry_recv,
+    relay_send,
+    relay_recv,
 ):
     frames, strip, width, channels = lat.shape
     row = lax.axis_index("rows")
@@ -51,9 +55,6 @@
     load_lat = pltpu.make_async_copy(lat_hbm, lat, load_sem.at[0])
     load_win = pltpu.make_async_copy(win_hbm, win, load_sem.at[1])
     load_wout = pltpu.make_async_copy(wout_hbm, wout, load_sem.at[2])
-    load_lat.start()
-    load_win.start()
-    load_wout.start()
 
     barrier = pltpu.get_barrier_semaphore()
     near = (
@@ -70,6 +71,9 @@
         def _():
             pl.semaphore_signal(barrier, inc=1, device_id=where, device_id_type=MESH)
 
+    load_lat.start()
+    load_win.start()
+    load_wout.start()
     pl.semaphore_wait(barrier, total)
 
     def halo_copy(side):
@@ -96,6 +100,19 @@
             device_id_type=MESH,
         )
 
+    def relay_copy(side, piece):
+        part = pl.ds(piece * span, span)
+        edge = strip - 1 if side == 0 else 0
+        target = row + 1 if side == 0 else row - 1
+        return pltpu.make_async_remote_copy(
+            src_ref=carry.at[edge, part],
+            dst_ref=relayed.at[side, part],
+            send_sem=relay_send.at[side, piece],
+            recv_sem=relay_recv.at[side, piece],
+            device_id={"rows": target},
+            device_id_type=MESH,
+        )
+
     def carry_copy(i, piece):
         part = pl.ds(piece * span, span)
         return pltpu.make_async_remote_copy(
@@ -133,44 +150,29 @@
         target[place, frame, :, channels : 2 * channels] = value
         target[place, frame, :, 2 * channels : 3 * channels] = after.astype(jnp.bfloat16)
 
-    def border(target, place, buffer, side, exists, arrival):
+    def border(i, side, exists):
         @pl.when(exists)
         def _():
-            arrival.wait_recv()
+            halo_copy(side).wait_recv()
             for frame in range(frames):
-                spread(target, place, frame, buffer[side, frame])
+                spread(wide, i, frame, halo[side, frame])
 
         @pl.when(jnp.logical_not(exists))
         def _():
-            target[place] = jnp.zeros(target.shape[1:], target.dtype)
-
-    def convolve(source, weight, i):
-        window = jnp.concatenate([source[i], source[i + 1], source[i + 2]], axis=-1)
+            wide[i] = jnp.zeros(wide.shape[1:], wide.dtype)
+
+    def drive(i):
+        window = jnp.concatenate([wide[i], wide[i + 1], wide[i + 2]], axis=-1)
         flat = window.reshape(frames * width, 9 * channels)
-        return jnp.dot(flat, weight[...], preferred_element_type=jnp.float32).reshape(
+        driven = jnp.dot(flat, win[...], preferred_element_type=jnp.float32).reshape(
             frames, width, channels
         )
-
-    def drive(i):
-        driven = convolve(wide, win, i)
         running = driven[0]
         partial[i, 0] = running
         for frame in range(1, frames):
             running = decays * running + driven[frame]
             partial[i, frame] = running
 
-    def publish(i):
-        for side, edge in ((0, strip - 1), (1, 0)):
-            if i == edge:
-
-                @pl.when(has_down if side == 0 else has_up)
-                def _():
-                    state_copy(side).start()
-
-        for frame in range(frames):
-            spread(wide_states, i + 1, frame, rounded[i, frame])
-
-    def first(i):
         @pl.when(jnp.logical_not(has_before))
         def _():
             passed[i] = partial[i, frames - 1].astype(passed.dtype)
@@ -180,63 +182,170 @@
                 for piece in range(PIECES):
                     carry_copy(i, piece).start()
 
-            for frame in range(frames):
-                rounded[i, frame] = partial[i, frame].astype(jnp.bfloat16)
-            publish(i)
-
-    def later(i):
-        @pl.when(has_before)
-        def _():
-            for piece in range(PIECES):
-                part = pl.ds(piece * span, span)
-                carry_copy(i, piece).wait_recv()
-                arrived = carry[i, part].astype(jnp.float32)
-                last = partial[i, frames - 1, part] + growth[frames - 1] * arrived
-                passed[i, part] = last.astype(passed.dtype)
-
-                @pl.when(has_after)
+    def settle(i, side, exists):
+        for frame in range(frames):
+            rounded[i, frame] = partial[i, frame].astype(jnp.bfloat16)
+
+        @pl.when(exists)
+        def _():
+            state_copy(side).start()
+
+    def advance(i, side=None, exists=None):
+        for piece in range(PIECES):
+            part = pl.ds(piece * span, span)
+            carry_copy(i, piece).wait_recv()
+            if side is not None:
+
+                @pl.when(exists)
                 def _():
-                    carry_copy(i, piece).start()
-
-                rounded[i, frames - 1, part] = last.astype(jnp.bfloat16)
-                for frame in range(frames - 1):
-                    state = partial[i, frame, part] + growth[frame] * arrived
-                    rounded[i, frame, part] = state.astype(jnp.bfloat16)
-            publish(i)
-
-    def emit(i):
-        mixed = convolve(wide_states, wout, i)
+                    relay_copy(side, piece).start()
+
+            arrived = carry[i, part].astype(jnp.float32)
+            last = partial[i, frames - 1, part] + growth[frames - 1] * arrived
+            passed[i, part] = last.astype(passed.dtype)
+
+            @pl.when(has_after)
+            def _():
+                carry_copy(i, piece).start()
+
+            partial[i, frames - 1, part] = last
+            for frame in range(frames - 1):
+                partial[i, frame, part] = partial[i, frame, part] + growth[frame] * arrived
+
+    def stretch(i):
         for frame in range(frames):
-            updated = lat[frame, i].astype(jnp.float32) + jax.nn.gelu(mixed[frame])
+            spread(wide_states, i + 1, frame, partial[i, frame].astype(jnp.bfloat16))
+
+    def outer(place, side, exists):
+        @pl.when(exists)
+        def _():
+            state_copy(side).wait_recv()
+
+            @pl.when(has_before)
+            def _():
+                for piece in range(PIECES):
+                    relay_copy(side, piece).wait_recv()
+                arrived = relayed[side].astype(jnp.float32)
+                for frame in range(frames):
+                    state = state_halo[side, frame].astype(jnp.float32)
+                    state = state + growth[frame] * arrived
+                    spread(wide_states, place, frame, state.astype(jnp.bfloat16))
+
+            @pl.when(jnp.logical_not(has_before))
+            def _():
+                for frame in range(frames):
+                    spread(wide_states, place, frame, state_halo[side, frame])
+
+    def product(i, low, high):
+        window = [wide_states[i + tap] for tap in range(low, high)]
+        window = window[0] if high == low + 1 else jnp.concatenate(window, axis=-1)
+        flat = window.reshape(frames * width, (high - low) * 3 * channels)
+        taps = wout[low * 3 * channels : high * 3 * channels]
+        value = jnp.dot(flat, taps, preferred_element_type=jnp.float32)
+        return value.reshape(frames, width, channels)
+
+    def write(i, value):
+        for frame in range(frames):
+            updated = lat[frame, i].astype(jnp.float32) + jax.nn.gelu(value[frame])
             result[frame, i] = updated.astype(jnp.bfloat16)
         pltpu.make_async_copy(result.at[:, i], out_hbm.at[:, i], store_sem.at[i]).start()
 
+    def close(side, exists):
+        i, place, low = (0, 0, 0) if side == 0 else (strip - 1, strip + 1, 2)
+        outer(place, side, exists)
+
+        @pl.when(exists)
+        def _():
+            write(i, mixed[side] + product(i, low, low + 1))
+
+        @pl.when(jnp.logical_not(exists))
+        def _():
+            write(i, mixed[side])
+
     middle = list(range(1, strip - 1))
-    edges = [0, strip - 1]
+    bottom = strip - 1
 
     load_lat.wait()
     for i in range(strip):
         for frame in range(frames):
             spread(wide, i + 1, frame, lat[frame, i])
     load_win.wait()
+    even = lax.rem(row, 2) == 0
+
+    def drive_top():
+        border(0, 0, has_up)
+        drive(0)
+        settle(0, 1, has_up)
+
+    def drive_bottom():
+        border(strip + 1, 1, has_down)
+        drive(bottom)
+        settle(bottom, 0, has_down)
+
+    def by_parity(one, two):
+        @pl.when(even)
+        def _():
+            one()
+
+        @pl.when(jnp.logical_not(even))
+        def _():
+            two()
+
+    for i in middle[:1]:
+        drive(i)
+    by_parity(drive_bottom, drive_top)
+    by_parity(drive_top, drive_bottom)
+    for i in middle[1:]:
+        drive(i)
+
+    @pl.when(has_before)
+    def _():
+        for i in middle[:1]:
+            advance(i)
+        for i in middle[:1]:
+            stretch(i)
+
+        def low_first():
+            advance(bottom, 0, has_down)
+            advance(0, 1, has_up)
+
+        def high_first():
+            advance(0, 1, has_up)
+            advance(bottom, 0, has_down)
+
+        by_parity(low_first, high_first)
+
+    load_wout.wait()
+
+    @pl.when(jnp.logical_not(has_before))
+    def _():
+        for i in middle[:1]:
+            stretch(i)
+
+    stretch(0)
+    stretch(bottom)
+    mixed[0] = product(0, 1, 3)
+
+    @pl.when(has_before)
+    def _():
+        for i in middle[1:]:
+            advance(i)
+
+    for i in middle[1:]:
+        stretch(i)
+    mixed[1] = product(bottom, 0, 2)
     for i in middle:
-        drive(i)
-        first(i)
-    border(wide, 0, halo, 0, has_up, halo_copy(0))
-    drive(0)
-    first(0)
-    border(wide, strip + 1, halo, 1, has_down, halo_copy(1))
-    drive(strip - 1)
-    first(strip - 1)
-    load_wout.wait()
-    for i in middle + edges:
-        later(i)
-    for i in middle:
-        emit(i)
-    border(wide_states, 0, state_halo, 0, has_up, state_copy(0))
-    emit(0)
-    border(wide_states, strip + 1, state_halo, 1, has_down, state_copy(1))
-    emit(strip - 1)
+        write(i, product(i, 0, 3))
+
+    def top_last():
+        close(1, has_down)
+        close(0, has_up)
+
+    def bottom_last():
+        close(0, has_up)
+        close(1, has_down)
+
+    by_parity(top_last, bottom_last)
 
     @pl.when(has_down)
     def _():
@@ -247,6 +356,16 @@
     def _():
         halo_copy(1).wait_send()
         state_copy(1).wait_send()
+
+    @pl.when(jnp.logical_and(has_down, has_before))
+    def _():
+        for piece in range(PIECES):
+            relay_copy(0, piece).wait_send()
+
+    @pl.when(jnp.logical_and(has_up, has_before))
+    def _():
+        for piece in range(PIECES):
+            relay_copy(1, piece).wait_send()
 
     @pl.when(has_after)
     def _():
@@ -286,6 +405,8 @@
             pltpu.VMEM((strip, width, channels), link),
             pltpu.VMEM((strip, frames, width, channels), half),
             pltpu.VMEM((2, frames, width, channels), half),
+            pltpu.VMEM((2, width, channels), link),
+            pltpu.VMEM((2, frames, width, channels), jnp.float32),
             pltpu.VMEM((strip + 2, frames, width, 3 * channels), half),
             pltpu.VMEM((frames, strip, width, channels), half),
             dma((3,)),
@@ -296,6 +417,8 @@
             dma((2,)),
             dma((strip, PIECES)),
             dma((strip, PIECES)),
+            dma((2, PIECES)),
+            dma((2, PIECES)),
         ],
         compiler_params=pltpu.CompilerParams(collective_id=0, has_side_effects=True),
     )(

time: 23.8 us -> 21.6 us (0.908)
  the two profiles are of different devices: /device:TPU:26 before, /device:TPU:25 now
where the time goes in v3:
time: 21.6 us; the launch traced here: 21.4 us
  Pallas kernels  19.6 us (91%)
  local copies, waits for them, and re-layouts  1.87 us (9%)
    pallas_call x1, Pallas kernels, local(): pl.pallas_call(functools.partial(kernel, positions, strips), out_shape=ja...  19.6 us
    unnamed x1, local copies, waits for them, and re-layouts  1.87 us

profile of v3, /device:TPU:25, one launch (start us, length us, event | category | flops | bytes accessed | tf_op | source)
XLA Modules:
  0.0 21.4 jit_solution(6895656928173530228)
XLA Ops:
  0.0 19.6 %shard_map.55 = bf16[2,4,128,256]{3,2,1,0:T(8,128)(2,1)} custom-call(bf16[2,4,128,256]{3,2,1,0:T(8,128)(2,1)} %lat_hbm.1, bf16[2304,256]{1,0:T(8,128)(2,1)} %bitcast.3, bf16[2304,256]{1,0:T(8,128)(2,1)} %bitcast.4, f32[16]{0:T(128)} %table_ref.1, s32[1,256]{1,0:T(1,128)} %bitcast.5), custom_call_target="tpu_custom_call" | custom-call | tf_op jit(solution)/shard_map/pallas_call | solution.py:386
  19.6 1.9 %copy.7 = bf16[2,4,128,256]{3,2,1,0:T(8,128)(2,1)} copy(bf16[2,4,128,256]{3,2,1,0:T(8,128)(2,1)} %shard_map.55) | data formatting | bytes 1048576

commit v4 on v3

--- a/solution.py
+++ b/solution.py
@@ -8,7 +8,7 @@
 from jax.sharding import PartitionSpec as P
 
 MESH = pl.DeviceIdType.MESH
-PIECES = 2
+PIECES = 4
 
 
 def kernel(
@@ -124,11 +124,17 @@
             device_id_type=MESH,
         )
 
+    even = lax.rem(row, 2) == 0
+
+    @pl.when(jnp.logical_and(has_up, even))
+    def _():
+        halo_copy(1).start()
+
     @pl.when(has_down)
     def _():
         halo_copy(0).start()
 
-    @pl.when(has_up)
+    @pl.when(jnp.logical_and(has_up, jnp.logical_not(even)))
     def _():
         halo_copy(1).start()
 
@@ -270,7 +276,6 @@
         for frame in range(frames):
             spread(wide, i + 1, frame, lat[frame, i])
     load_win.wait()
-    even = lax.rem(row, 2) == 0
 
     def drive_top():
         border(0, 0, has_up)

time: 21.6 us -> 21.2 us (0.981)
  Pallas kernels: 19.6 us -> 19.2 us
    pallas_call x1, Pallas kernels: 19.6 us -> 19.2 us  [local(): pl.pallas_call(functools.partial(kernel, positions, strips), out_shape=ja...]
where the time goes in v4:
time: 21.2 us; the launch traced here: 21.1 us
  Pallas kernels  19.2 us (91%)
  local copies, waits for them, and re-layouts  1.87 us (9%)
    pallas_call x1, Pallas kernels, local(): pl.pallas_call(functools.partial(kernel, positions, strips), out_shape=ja...  19.2 us
    unnamed x1, local copies, waits for them, and re-layouts  1.87 us

profile of v4, /device:TPU:25, one launch (start us, length us, event | category | flops | bytes accessed | tf_op | source)
XLA Modules:
  0.0 21.1 jit_solution(1925190128439427054)
XLA Ops:
  0.0 19.2 %shard_map.55 = bf16[2,4,128,256]{3,2,1,0:T(8,128)(2,1)} custom-call(bf16[2,4,128,256]{3,2,1,0:T(8,128)(2,1)} %lat_hbm.1, bf16[2304,256]{1,0:T(8,128)(2,1)} %bitcast.3, bf16[2304,256]{1,0:T(8,128)(2,1)} %bitcast.4, f32[16]{0:T(128)} %table_ref.1, s32[1,256]{1,0:T(1,128)} %bitcast.5), custom_call_target="tpu_custom_call" | custom-call | tf_op jit(solution)/shard_map/pallas_call | solution.py:391
  19.2 1.9 %copy.7 = bf16[2,4,128,256]{3,2,1,0:T(8,128)(2,1)} copy(bf16[2,4,128,256]{3,2,1,0:T(8,128)(2,1)} %shard_map.55) | data formatting | bytes 1048576

commit v5 on v4

--- a/solution.py
+++ b/solution.py
@@ -17,8 +17,8 @@
     lat_hbm,
     win_hbm,
     wout_hbm,
-    table_ref,
-    index_ref,
+    table_hbm,
+    index_hbm,
     out_hbm,
     lat,
     win,
@@ -32,6 +32,8 @@
     state_halo,
     relayed,
     mixed,
+    table_ref,
+    index_ref,
     wide_states,
     result,
     load_sem,
@@ -55,6 +57,8 @@
     load_lat = pltpu.make_async_copy(lat_hbm, lat, load_sem.at[0])
     load_win = pltpu.make_async_copy(win_hbm, win, load_sem.at[1])
     load_wout = pltpu.make_async_copy(wout_hbm, wout, load_sem.at[2])
+    load_table = pltpu.make_async_copy(table_hbm, table_ref, load_sem.at[3])
+    load_index = pltpu.make_async_copy(index_hbm, index_ref, load_sem.at[4])
 
     barrier = pltpu.get_barrier_semaphore()
     near = (
@@ -72,6 +76,8 @@
             pl.semaphore_signal(barrier, inc=1, device_id=where, device_id_type=MESH)
 
     load_lat.start()
+    load_table.start()
+    load_index.start()
     load_win.start()
     load_wout.start()
     pl.semaphore_wait(barrier, total)
@@ -138,6 +144,8 @@
     def _():
         halo_copy(1).start()
 
+    load_table.wait()
+    load_index.wait()
     chosen = index_ref[...]
     decays = jnp.zeros(chosen.shape, jnp.float32)
     for level in range(table_ref.shape[0]):
@@ -395,8 +403,8 @@
             anywhere,
             anywhere,
             anywhere,
-            pl.BlockSpec(memory_space=pltpu.SMEM),
-            pl.BlockSpec(memory_space=pltpu.VMEM),
+            anywhere,
+            anywhere,
         ],
         out_specs=anywhere,
         scratch_shapes=[
@@ -412,9 +420,11 @@
             pltpu.VMEM((2, frames, width, channels), half),
             pltpu.VMEM((2, width, channels), link),
             pltpu.VMEM((2, frames, width, channels), jnp.float32),
+            pltpu.SMEM(decay_table.shape, jnp.float32),
+            pltpu.VMEM((1, channels), jnp.int32),
             pltpu.VMEM((strip + 2, frames, width, 3 * channels), half),
             pltpu.VMEM((frames, strip, width, channels), half),
-            dma((3,)),
+            dma((5,)),
             dma((strip,)),
             dma((2,)),
             dma((2,)),
@@ -425,13 +435,13 @@
             dma((2, PIECES)),
             dma((2, PIECES)),
         ],
-        compiler_params=pltpu.CompilerParams(collective_id=0, has_side_effects=True),
+        compiler_params=pltpu.CompilerParams(collective_id=0, has_side_effects=True, vmem_limit_bytes=32 * 1024 * 1024),
     )(
-        latents,
-        weight_in.reshape(9 * channels, channels),
-        weight_out.reshape(9 * channels, channels),
-        decay_table,
-        decay_index.reshape(1, channels),
+        pltpu.with_memory_space_constraint(latents, pltpu.HBM),
+        pltpu.with_memory_space_constraint(weight_in.reshape(9 * channels, channels), pltpu.HBM),
+        pltpu.with_memory_space_constraint(weight_out.reshape(9 * channels, channels), pltpu.HBM),
+        pltpu.with_memory_space_constraint(decay_table, pltpu.HBM),
+        pltpu.with_memory_space_constraint(decay_index.reshape(1, channels), pltpu.HBM),
     )
 
 

time: 21.2 us -> 19.4 us (0.915)
  local copies, waits for them, and re-layouts: 1.87 us -> 0.8 us
  Pallas kernels: 19.2 us -> 18.5 us
    unnamed x1, local copies, waits for them, and re-layouts: 1.87 us -> 0.8 us
    pallas_call x1, Pallas kernels: 19.2 us -> 18.5 us  [local(): pl.pallas_call(functools.partial(kernel, positions, strips), out_shape=ja...]
where the time goes in v5:
time: 19.4 us; the launch traced here: 19.3 us
  Pallas kernels  18.5 us (95%)
  local copies, waits for them, and re-layouts  0.8 us (4%)
    pallas_call x1, Pallas kernels, local(): pl.pallas_call(functools.partial(kernel, positions, strips), out_shape=ja...  18.5 us
    unnamed x1, local copies, waits for them, and re-layouts  0.8 us

profile of v5, /device:TPU:25, one launch (start us, length us, event | category | flops | bytes accessed | tf_op | source)
XLA Modules:
  0.0 19.3 jit_solution(10223820783321284916)
XLA Ops:
  0.0 18.5 %shard_map.55 = bf16[2,4,128,256]{3,2,1,0:T(8,128)(2,1)S(1)} custom-call(bf16[2,4,128,256]{3,2,1,0:T(8,128)(2,1)} %lat_hbm.1, bf16[2304,256]{1,0:T(8,128)(2,1)} %bitcast.3, bf16[2304,256]{1,0:T(8,128)(2,1)} %bitcast.4, f32[16]{0:T(128)} %table_hbm.1, s32[1,256]{1,0:T(1,128)} %bitcast.5), custom_call_target="tpu_custom_call" | custom-call | tf_op jit(solution)/shard_map/pallas_call | solution.py:399
  18.5 0.8 %copy.7 = bf16[2,4,128,256]{3,2,1,0:T(8,128)(2,1)} copy(bf16[2,4,128,256]{3,2,1,0:T(8,128)(2,1)S(1)} %shard_map.55) | data formatting | bytes 1048576

commit v6 on v5

--- a/solution.py
+++ b/solution.py
@@ -187,6 +187,7 @@
             running = decays * running + driven[frame]
             partial[i, frame] = running
 
+    def begin(i):
         @pl.when(jnp.logical_not(has_before))
         def _():
             passed[i] = partial[i, frames - 1].astype(passed.dtype)
@@ -197,6 +198,7 @@
                     carry_copy(i, piece).start()
 
     def settle(i, side, exists):
+        begin(i)
         for frame in range(frames):
             rounded[i, frame] = partial[i, frame].astype(jnp.bfloat16)
 
@@ -250,12 +252,14 @@
                 for frame in range(frames):
                     spread(wide_states, place, frame, state_halo[side, frame])
 
-    def product(i, low, high):
-        window = [wide_states[i + tap] for tap in range(low, high)]
-        window = window[0] if high == low + 1 else jnp.concatenate(window, axis=-1)
-        flat = window.reshape(frames * width, (high - low) * 3 * channels)
-        taps = wout[low * 3 * channels : high * 3 * channels]
-        value = jnp.dot(flat, taps, preferred_element_type=jnp.float32)
+    def product(i, taps):
+        window = [wide_states[i + tap] for tap in taps]
+        window = window[0] if len(taps) == 1 else jnp.concatenate(window, axis=-1)
+        flat = window.reshape(frames * width, len(taps) * 3 * channels)
+        depth = 3 * channels
+        rows = [wout[tap * depth : (tap + 1) * depth] for tap in taps]
+        rows = rows[0] if len(taps) == 1 else jnp.concatenate(rows, axis=0)
+        value = jnp.dot(flat, rows, preferred_element_type=jnp.float32)
         return value.reshape(frames, width, channels)
 
     def write(i, value):
@@ -270,11 +274,11 @@
 
         @pl.when(exists)
         def _():
-            write(i, mixed[side] + product(i, low, low + 1))
+            write(i, mixed[i] + product(i, [low]))
 
         @pl.when(jnp.logical_not(exists))
         def _():
-            write(i, mixed[side])
+            write(i, mixed[i])
 
     middle = list(range(1, strip - 1))
     bottom = strip - 1
@@ -304,20 +308,32 @@
         def _():
             two()
 
+    late = middle[1:]
+    early = moment == 1
+
     for i in middle[:1]:
         drive(i)
+        begin(i)
     by_parity(drive_bottom, drive_top)
-    by_parity(drive_top, drive_bottom)
-    for i in middle[1:]:
+    for i in late:
         drive(i)
 
-    @pl.when(has_before)
+    @pl.when(early)
     def _():
         for i in middle[:1]:
             advance(i)
+
+    by_parity(drive_top, drive_bottom)
+    for i in late:
+        begin(i)
+
+    @pl.when(jnp.logical_and(has_before, jnp.logical_not(early)))
+    def _():
         for i in middle[:1]:
-            stretch(i)
-
+            advance(i)
+
+    @pl.when(has_before)
+    def _():
         def low_first():
             advance(bottom, 0, has_down)
             advance(0, 1, has_up)
@@ -328,27 +344,32 @@
 
         by_parity(low_first, high_first)
 
+    @pl.when(jnp.logical_and(has_before, has_after))
+    def _():
+        for i in late:
+            advance(i)
+
     load_wout.wait()
-
-    @pl.when(jnp.logical_not(has_before))
-    def _():
-        for i in middle[:1]:
-            stretch(i)
-
-    stretch(0)
-    stretch(bottom)
-    mixed[0] = product(0, 1, 3)
-
-    @pl.when(has_before)
-    def _():
-        for i in middle[1:]:
+    ready = [i for i in range(strip) if i not in late]
+    for i in ready:
+        stretch(i)
+    for i in range(strip):
+        taps = [tap for tap in range(3) if i + tap - 1 in ready]
+        mixed[i] = product(i, taps) if taps else jnp.zeros(mixed.shape[1:], jnp.float32)
+
+    @pl.when(jnp.logical_and(has_before, jnp.logical_not(has_after)))
+    def _():
+        for i in late:
             advance(i)
 
-    for i in middle[1:]:
+    for i in late:
         stretch(i)
-    mixed[1] = product(bottom, 0, 2)
-    for i in middle:
-        write(i, product(i, 0, 3))
+    for i in range(strip):
+        taps = [tap for tap in range(3) if i + tap - 1 in late]
+        if i in middle:
+            write(i, mixed[i] + product(i, taps) if taps else mixed[i])
+        elif taps:
+            mixed[i] = mixed[i] + product(i, taps)
 
     def top_last():
         close(1, has_down)
@@ -419,7 +440,7 @@
             pltpu.VMEM((strip, frames, width, channels), half),
             pltpu.VMEM((2, frames, width, channels), half),
             pltpu.VMEM((2, width, channels), link),
-            pltpu.VMEM((2, frames, width, channels), jnp.float32),
+            pltpu.VMEM((strip, frames, width, channels), jnp.float32),
             pltpu.SMEM(decay_table.shape, jnp.float32),
             pltpu.VMEM((1, channels), jnp.int32),
             pltpu.VMEM((strip + 2, frames, width, 3 * channels), half),

time: 19.4 us -> 18.3 us (0.943)
  Pallas kernels: 18.5 us -> 17.3 us
    pallas_call x1, Pallas kernels: 18.5 us -> 17.3 us  [local(): pl.pallas_call(functools.partial(kernel, positions, strips), out_shape=ja...]
where the time goes in v6:
time: 18.3 us; the launch traced here: 18.1 us
  Pallas kernels  17.3 us (95%)
  local copies, waits for them, and re-layouts  0.8 us (4%)
    pallas_call x1, Pallas kernels, local(): pl.pallas_call(functools.partial(kernel, positions, strips), out_shape=ja...  17.3 us
    unnamed x1, local copies, waits for them, and re-layouts  0.8 us

profile of v6, /device:TPU:25, one launch (start us, length us, event | category | flops | bytes accessed | tf_op | source)
XLA Modules:
  0.0 18.1 jit_solution(9766474896613346357)
XLA Ops:
  0.0 17.3 %shard_map.55 = bf16[2,4,128,256]{3,2,1,0:T(8,128)(2,1)S(1)} custom-call(bf16[2,4,128,256]{3,2,1,0:T(8,128)(2,1)} %lat_hbm.1, bf16[2304,256]{1,0:T(8,128)(2,1)} %bitcast.3, bf16[2304,256]{1,0:T(8,128)(2,1)} %bitcast.4, f32[16]{0:T(128)} %table_hbm.1, s32[1,256]{1,0:T(1,128)} %bitcast.5), custom_call_target="tpu_custom_call" | custom-call | tf_op jit(solution)/shard_map/pallas_call | solution.py:420
  17.3 0.8 %copy.7 = bf16[2,4,128,256]{3,2,1,0:T(8,128)(2,1)} copy(bf16[2,4,128,256]{3,2,1,0:T(8,128)(2,1)S(1)} %shard_map.55) | data formatting | bytes 1048576

commit v7 on v6

--- a/solution.py
+++ b/solution.py
@@ -8,7 +8,7 @@
 from jax.sharding import PartitionSpec as P
 
 MESH = pl.DeviceIdType.MESH
-PIECES = 4
+PIECES = 8
 
 
 def kernel(

time: 18.3 us -> 18.5 us (1.011)
  Pallas kernels: 17.3 us -> 17.6 us
    pallas_call x1, Pallas kernels: 17.3 us -> 17.6 us  [local(): pl.pallas_call(functools.partial(kernel, positions, strips), out_shape=ja...]
where the time goes in v7:
time: 18.5 us; the launch traced here: 18.4 us
  Pallas kernels  17.6 us (95%)
  local copies, waits for them, and re-layouts  0.8 us (4%)
    pallas_call x1, Pallas kernels, local(): pl.pallas_call(functools.partial(kernel, positions, strips), out_shape=ja...  17.6 us
    unnamed x1, local copies, waits for them, and re-layouts  0.8 us

profile of v7, /device:TPU:25, one launch (start us, length us, event | category | flops | bytes accessed | tf_op | source)
XLA Modules:
  0.0 18.4 jit_solution(18319692439764766714)
XLA Ops:
  0.0 17.6 %shard_map.55 = bf16[2,4,128,256]{3,2,1,0:T(8,128)(2,1)S(1)} custom-call(bf16[2,4,128,256]{3,2,1,0:T(8,128)(2,1)} %lat_hbm.1, bf16[2304,256]{1,0:T(8,128)(2,1)} %bitcast.3, bf16[2304,256]{1,0:T(8,128)(2,1)} %bitcast.4, f32[16]{0:T(128)} %table_hbm.1, s32[1,256]{1,0:T(1,128)} %bitcast.5), custom_call_target="tpu_custom_call" | custom-call | tf_op jit(solution)/shard_map/pallas_call | solution.py:420
  17.6 0.8 %copy.7 = bf16[2,4,128,256]{3,2,1,0:T(8,128)(2,1)} copy(bf16[2,4,128,256]{3,2,1,0:T(8,128)(2,1)S(1)} %shard_map.55) | data formatting | bytes 1048576
